TPU v7x, 512 devices: a whole 4x8x8 slice. The times are simulated.
512 devices in a mesh: dp: 64 (over z_lo, y, x), tensor: 8 (over z_hi, core).
Axes of the slice: x: 4, y: 8, z: 8 (z_hi: 4, z_lo: 2; z = z_hi * 2 + z_lo), core: 2. Of those that a mesh axis runs over, the one named last changes fastest.
Arguments:
- tokens: bfloat16 [8192, 6144], P('dp', 'tensor'), may hold values from -6 to 6
- cotangent: bfloat16 [8192, 6144], P('dp', 'tensor'), may hold values from -6 to 6
- w_gate: bfloat16 [1, 6144, 16384], P(None, 'tensor', 'dp'), may hold values from -0.078125 to 0.078125
- w_up: bfloat16 [1, 6144, 16384], P(None, 'tensor', 'dp'), may hold values from -0.078125 to 0.078125
- w_down: bfloat16 [1, 16384, 6144], P(None, 'dp', 'tensor'), may hold values from -0.046875 to 0.046875
- slot_token: int32 [64, 1, 6], P('dp'), may hold values from -1 to 127, as said below
- route_weight: float32 [64, 1, 6], P('dp'), may hold values from 0.2 to 1
Outputs:
- mixed: bfloat16 [8192, 6144], P('dp', 'tensor')
- grad_tokens: bfloat16 [8192, 6144], P('dp', 'tensor')
- grad_gate: bfloat16 [1, 6144, 16384], P(None, 'tensor', 'dp')
- grad_up: bfloat16 [1, 6144, 16384], P(None, 'tensor', 'dp')
- grad_down: bfloat16 [1, 16384, 6144], P(None, 'dp', 'tensor')
Inputs may be any that keep to these rules, and one draw needn't show every extreme that they name: `slot_token`: for each block and expert the filled slots come first and name distinct tokens of that block; every block has at least one filled slot for each expert, and for each expert some block fills all 6 slots.
All inputs are finite; a program needn't handle non-finite values.
Results may differ from a plain program's by a relative error of at most 0.0057.
Values may be sent and summed in bfloat16 or wider, within the bound.
No kernel may reach another device: no remote copies, remote signals or barrier semaphores. Data moves between devices by JAX's collectives and lax.ppermute only.
A program may use at most 64 MiB of HBM per device.

v0:
```python
import jax
import jax.numpy as jnp
from jax import lax
from jax.sharding import PartitionSpec as P


def on_device(tokens, cotangent, w_gate, w_up, w_down, slot_token, route_weight):
    tok_dev = tokens.shape[0]
    slot_ids = slot_token[0].T
    slot_weights = route_weight[0].T
    usable = slot_ids >= 0
    clipped = jnp.maximum(slot_ids, 0)
    picked = jnp.where(usable[:, :, None], tokens[clipped], 0)
    d_local = (
        slot_weights[:, :, None]
        * cotangent[clipped].astype(jnp.float32)
        * usable[:, :, None].astype(jnp.float32)
    ).astype(jnp.bfloat16)
    all_rows = lax.all_gather(picked, "dp", axis=0, tiled=True)
    gate_part = jnp.einsum("sed,edf->sef", all_rows, w_gate, preferred_element_type=jnp.float32)
    up_part = jnp.einsum("sed,edf->sef", all_rows, w_up, preferred_element_type=jnp.float32)
    gate_sum, up_sum = lax.psum((gate_part, up_part), "tensor")
    sigmoid_gate = jax.nn.sigmoid(gate_sum)
    activated = gate_sum * sigmoid_gate
    hidden = (activated * up_sum).astype(jnp.bfloat16)
    local_combine = (jnp.arange(tok_dev, dtype=jnp.int32)[:, None, None] == slot_ids[None]).astype(
        jnp.float32
    )
    own_rows = lax.psum_scatter(
        jnp.einsum("sef,efd->sed", hidden, w_down, preferred_element_type=jnp.float32),
        "dp",
        scatter_dimension=0,
        tiled=True,
    )
    mixed = jnp.einsum(
        "tce,ced->td", local_combine * slot_weights[None], own_rows, precision=lax.Precision.HIGHEST
    )
    all_grads = lax.all_gather(d_local, "dp", axis=0, tiled=True)
    hidden_part = jnp.einsum("sed,efd->sef", all_grads, w_down, preferred_element_type=jnp.float32)
    hidden_grad = lax.psum(hidden_part, "tensor")
    d_gate = (hidden_grad * up_sum * sigmoid_gate * (1.0 + gate_sum * (1.0 - sigmoid_gate))).astype(
        jnp.bfloat16
    )
    d_up = (hidden_grad * activated).astype(jnp.bfloat16)
    grad_down = jnp.einsum(
        "sef,sed->efd", hidden, all_grads, preferred_element_type=jnp.float32
    ).astype(jnp.bfloat16)
    grad_gate = jnp.einsum(
        "sed,sef->edf", all_rows, d_gate, preferred_element_type=jnp.float32
    ).astype(jnp.bfloat16)
    grad_up = jnp.einsum("sed,sef->edf", all_rows, d_up, preferred_element_type=jnp.float32).astype(
        jnp.bfloat16
    )
    own_grads = lax.psum_scatter(
        jnp.einsum("sef,edf->sed", d_gate, w_gate, preferred_element_type=jnp.float32)
        + jnp.einsum("sef,edf->sed", d_up, w_up, preferred_element_type=jnp.float32),
        "dp",
        scatter_dimension=0,
        tiled=True,
    )
    grad_tokens = jnp.einsum(
        "tce,ced->td", local_combine, own_grads, precision=lax.Precision.HIGHEST
    )
    return (
        mixed.astype(jnp.bfloat16),
        grad_tokens.astype(jnp.bfloat16),
        grad_gate,
        grad_up,
        grad_down,
    )


def solution(mesh):
    return jax.shard_map(
        on_device,
        mesh=mesh,
        in_specs=(
            P("dp", "tensor"),
            P("dp", "tensor"),
            P(None, "tensor", "dp"),
            P(None, "tensor", "dp"),
            P(None, "dp", "tensor"),
            P("dp", None, None),
            P("dp", None, None),
        ),
        out_specs=(
            P("dp", "tensor"),
            P("dp", "tensor"),
            P(None, "tensor", "dp"),
            P(None, "tensor", "dp"),
            P(None, "dp", "tensor"),
        ),
        check_vma=False,
    )
```

profile of v0, /device:TPU:64, one launch (start us, length us, event | category | flops | bytes accessed | tf_op | source)
XLA Modules:
  0.0 1044.3 jit_solution(7480080014284035748)
XLA Ops:
  7.2 0.0 all-reduce.9.cloned.1.call-start
  7.2 0.7 maximum_bitcast_fusion
  7.9 0.7 fusion.37
  8.6 1.5 gather_fusion.1
  10.1 0.7 fusion.30
  10.9 1.5 gather_fusion
  12.4 0.1 bitcast_select_fusion
  12.5 161.2 %all_gather.7 = bf16[384,1,768]{2,1,0:T(2,128)(2,1)S(1)} all-gather(bf16[6,1,768]{2,1,0:T(2,128)(2,1)S(1)} %copy.18), channel_id=1, replica_groups=mesh['dp'=64,'tensor'=8] {'dp'}, dimensions={0}, use_global_device_ids=true | all-gather | bytes 599040 | tf_op jit(solution)/shard_map/all_gather | solution.py:38
  173.7 156.4 %all_gather.6 = bf16[384,1,768]{2,1,0:T(2,128)(2,1)S(1)} all-gather(bf16[6,1,768]{2,1,0:T(2,128)(2,1)S(1)} %copy.16), channel_id=1, replica_groups=mesh['dp'=64,'tensor'=8] {'dp'}, dimensions={0}, use_global_device_ids=true | all-gather | bytes 599040 | tf_op jit(solution)/shard_map/all_gather | solution.py:19
  330.1 0.1 copy.20
  330.2 0.9 copy-done.2
  331.1 1.1 convolution_bitcast_fusion.2
  332.2 1.1 convolution_bitcast_fusion.3
  333.2 1.1 convolution_bitcast_fusion.1
  334.3 0.0 all-reduce.9.cloned.1.call-update
  334.4 0.0 all-reduce.7.cloned.1.call-start
  334.4 81.8 %all-reduce.9.cloned.1.call-done = (f32[384,1,256]{2,0,1:T(8,128)}, f32[384,1,256]{2,0,1:T(8,128)}, f32[384,1,256]{2,0,1:T(8,128)}) async-done(((f32[384,1,256]{2,0,1:T(8,128)}, f32[384,1,256]{2,0,1:T(8,128)}, f32[384,1,256]{2,0,1:T(8,128)}), (f32[384,1,256]{2,0,1:T(8,128)}, f32[384,1,256]{2,0,1:T(8,128)}, f32[384,1,256]{2,0,1:T(8,128)})) %all-reduce.9.cloned.1.call-update) | async-done | bytes 1179664 | tf_op jit(solution)/shard_map/psum | solution.py:22
  416.2 1.5 fusion.21
  417.6 0.3 fusion.14
  418.0 0.3 fusion
  418.4 2.2 copy.19
  420.6 0.3 convolution_bitcast_fusion
  420.9 2.2 copy.17
  423.2 0.0 all-reduce.7.cloned.1.call-update
  423.2 1.3 dynamic-slice
  425.1 1.1 fusion.3
  426.2 1.2 fusion.2
  427.4 1.2 fusion.1
  428.6 605.9 %all-reduce.7.cloned.1.call-done = (f32[384,1,768]{2,1,0:T(1,128)}, f32[384,1,768]{2,1,0:T(1,128)}) async-done(((f32[384,1,768]{2,1,0:T(1,128)}, f32[384,1,768]{2,1,0:T(1,128)}), (f32[384,1,768]{2,1,0:T(1,128)}, f32[384,1,768]{2,1,0:T(1,128)})) %all-reduce.7.cloned.1.call-update) | async-done | bytes 2359312
  1034.4 0.7 constant_dynamic-slice_fusion
  1035.2 1.0 convolution_convert_fusion.3
  1036.2 1.3 convolution_convert_fusion.4
  (12 shorter events, 0.1 us)
Async XLA Ops:
  7.2 325.0 %copy-start = (bf16[1,768,256]{2,1,0:T(8,128)(2,1)S(1)}, bf16[1,768,256]{2,1,0:T(8,128)(2,1)}, u32[]{:S(2)}) copy-start(bf16[1,768,256]{2,1,0:T(8,128)(2,1)} %param.9) | copy-start | bytes 1179652
  7.2 409.0 %all-reduce.9.cloned.1.call-start = ((), (), s32[]{:S(2)}) async-start(), calls=%async_computation.1 | async-start | bytes 2359296 | tf_op jit(solution)/shard_map/psum | solution.py:22
  330.1 1.0 copy-start.2
  331.1 2.1 copy-start.1
  334.4 700.1 %all-reduce.7.cloned.1.call-start = ((), (), s32[]{:S(2)}) async-start(), calls=%async_computation | async-start | bytes 4718592
  426.2 608.9 %copy-start.3 = (s32[1,1,6]{2,1,0:T(1,128)S(1)}, s32[1,1,6]{2,1,0:T(1,128)}, u32[]{:S(2)}) copy-start(s32[1,1,6]{2,1,0:T(1,128)} %param.12) | copy-start | bytes 76
  426.2 609.9 %copy-start.4 = (f32[1,1,6]{2,1,0:T(1,128)S(1)}, f32[1,1,6]{2,1,0:T(1,128)}, u32[]{:S(2)}) copy-start(f32[1,1,6]{2,1,0:T(1,128)} %param.13) | copy-start | bytes 76
Sparse Core Ops, SparseCore 0:
  334.5 81.6 all-reduce.8
  423.3 611.0 all-reduce.6
where the time goes:
time: 1040 us
  waiting for transfers between devices  688 us (66%)
  blocking collectives  318 us (31%)
  between operations  14.8 us (1%)
  local copies, waits for them, and re-layouts  10.6 us (1%)
    unnamed x3, waiting for transfers between devices  606 us
    all_gather x1, blocking collectives, on_device(): all_grads = lax.all_gather(d_local, 'dp', axis=0, tiled=True)  161 us
    all_gather x1, blocking collectives, on_device(): all_rows = lax.all_gather(picked, 'dp', axis=0, tiled=True)  156 us
    psum x1, waiting for transfers between devices, on_device(): gate_sum, up_sum = lax.psum((gate_part, up_part), 'tensor')  81.8 us
  transfers between devices with their start and end apart: 2, of which 2 were waited for; matrix products, arithmetic and copies ran while one was open for 0% of the time, Pallas kernels for 0%

commit v1 on v0

--- a/solution.py
+++ b/solution.py
@@ -2,6 +2,15 @@
 import jax.numpy as jnp
 from jax import lax
 from jax.sharding import PartitionSpec as P
+
+
+def build_axis_part(row_data):
+    return jnp.concatenate(
+        lax.all_to_all(
+            jnp.stack([row_data] * lax.axis_size("dp")), axis_name="dp", split_axis=0, concat_axis=0
+        ),
+        axis=0,
+    )
 
 
 def on_device(tokens, cotangent, w_gate, w_up, w_down, slot_token, route_weight):
@@ -16,7 +25,7 @@
         * cotangent[clipped].astype(jnp.float32)
         * usable[:, :, None].astype(jnp.float32)
     ).astype(jnp.bfloat16)
-    all_rows = lax.all_gather(picked, "dp", axis=0, tiled=True)
+    all_rows = build_axis_part(picked)
     gate_part = jnp.einsum("sed,edf->sef", all_rows, w_gate, preferred_element_type=jnp.float32)
     up_part = jnp.einsum("sed,edf->sef", all_rows, w_up, preferred_element_type=jnp.float32)
     gate_sum, up_sum = lax.psum((gate_part, up_part), "tensor")

time: 1040 us -> 908 us (0.87)
  blocking collectives: 318 us -> 169 us
  starting transfers between devices: 0.08 us -> 11.9 us
    all_gather x1 -> x0, blocking collectives: 156 us -> none  [on_device(): all_rows = lax.all_gather(picked, 'dp', axis=0, tiled=True)]
    all_to_all x0 -> x1, starting transfers between devices: none -> 11.8 us  [build_axis_part(): lax.all_to_all(jnp.stack([row_data] * lax.axis_size('dp')), axis_name='dp...]
  transfers between devices with their start and end apart: 2 -> 3, of which waited for: 2 -> 2; matrix products, arithmetic and copies ran while one was open for 0% -> 1% of each run, Pallas kernels for 0% -> 0%
where the time goes in v1:
time: 908 us; the launch traced here: 907 us
  waiting for transfers between devices  687 us (76%)
  blocking collectives  169 us (19%)
  between operations  14.8 us (2%)
  starting transfers between devices  11.9 us (1%)
  matrix products  10.9 us (1%)
  local copies, waits for them, and re-layouts  10.4 us (1%)
    unnamed x3, waiting for transfers between devices  606 us
    all_gather x1, blocking collectives, on_device(): all_grads = lax.all_gather(d_local, 'dp', axis=0, tiled=True)  169 us
    psum x1, waiting for transfers between devices, on_device(): gate_sum, up_sum = lax.psum((gate_part, up_part), 'tensor')  81.1 us
  transfers between devices with their start and end apart: 3, of which 2 were waited for; matrix products, arithmetic and copies ran while one was open for 1% of the time, Pallas kernels for 0%

profile of v1, /device:TPU:64, one launch (start us, length us, event | category | flops | bytes accessed | tf_op | source)
XLA Modules:
  0.0 907.4 jit_solution(9491850191794851445)
XLA Ops:
  7.2 0.7 maximum_bitcast_fusion
  7.9 0.7 fusion.33
  8.6 1.5 gather_fusion
  10.1 0.1 broadcast_select_fusion
  10.2 1.0 stack.2
  11.1 11.8 %all-to-all-start = ((bf16[64,6,1,768]{3,1,2,0:T(8,128)(2,1)}), bf16[64,6,1,768]{3,1,2,0:T(8,128)(2,1)S(1)}, u32[]{:S(2)}, u32[]{:S(2)}) async-start(bf16[64,6,1,768]{3,1,2,0:T(8,128)(2,1)} %stack.2), calls=%async_computation | async-start | bytes 1572864 | tf_op jit(solution)/shard_map/all_to_all | solution.py:9
  22.9 0.0 all-reduce.9.cloned.1.call-start
  23.0 0.6 gather_fusion.1
  23.6 0.1 fusion.26
  23.7 169.3 %all_gather.3 = bf16[384,1,768]{2,1,0:T(2,128)(2,1)S(1)} all-gather(bf16[6,1,768]{2,1,0:T(2,128)(2,1)S(1)} %copy.16), channel_id=1, replica_groups=mesh['dp'=64,'tensor'=8] {'dp'}, dimensions={0}, use_global_device_ids=true | all-gather | bytes 599040 | tf_op jit(solution)/shard_map/all_gather | solution.py:47
  193.0 1.1 convolution_bitcast_fusion.1
  194.1 0.2 reshape.299
  194.3 2.1 convolution_bitcast_fusion.2
  196.4 1.1 convolution_bitcast_fusion.3
  197.5 0.0 all-reduce.9.cloned.1.call-update
  197.5 0.0 all-reduce.7.cloned.1.call-start
  197.5 81.1 %all-reduce.9.cloned.1.call-done = (f32[384,1,256]{2,0,1:T(8,128)}, f32[384,1,256]{2,0,1:T(8,128)}, f32[384,1,256]{2,0,1:T(8,128)}) async-done(((f32[384,1,256]{2,0,1:T(8,128)}, f32[384,1,256]{2,0,1:T(8,128)}, f32[384,1,256]{2,0,1:T(8,128)}), (f32[384,1,256]{2,0,1:T(8,128)}, f32[384,1,256]{2,0,1:T(8,128)}, f32[384,1,256]{2,0,1:T(8,128)})) %all-reduce.9.cloned.1.call-update) | async-done | bytes 1179664 | tf_op jit(solution)/shard_map/psum | solution.py:31
  278.7 1.5 fusion.17
  280.2 0.3 fusion.10
  280.5 0.6 copy-done.2
  281.1 0.3 fusion
  281.5 2.2 copy.17
  283.7 0.3 convolution_bitcast_fusion
  284.1 2.2 copy.15
  286.3 1.3 dynamic-slice
  288.3 1.1 fusion.3
  289.4 1.2 fusion.2
  290.5 1.2 fusion.1
  291.7 605.9 %all-reduce.7.cloned.1.call-done = (f32[384,1,768]{2,1,0:T(1,128)}, f32[384,1,768]{2,1,0:T(1,128)}) async-done(((f32[384,1,768]{2,1,0:T(1,128)}, f32[384,1,768]{2,1,0:T(1,128)}), (f32[384,1,768]{2,1,0:T(1,128)}, f32[384,1,768]{2,1,0:T(1,128)})) %all-reduce.7.cloned.1.call-update) | async-done | bytes 2359312
  897.6 0.7 constant_dynamic-slice_fusion
  898.3 1.0 convolution_convert_fusion.3
  899.3 1.3 convolution_convert_fusion.4
  (15 shorter events, 0.1 us)
Async XLA Ops:
  7.2 189.2 %copy-start = (bf16[1,768,256]{2,1,0:T(8,128)(2,1)S(1)}, bf16[1,768,256]{2,1,0:T(8,128)(2,1)}, u32[]{:S(2)}) copy-start(bf16[1,768,256]{2,1,0:T(8,128)(2,1)} %param.9) | copy-start | bytes 1179652
  10.2 12.8 %copy-start.3 = (bf16[128,768]{1,0:T(8,128)(2,1)S(1)}, bf16[128,768]{1,0:T(8,128)(2,1)}, u32[]{:S(2)}) copy-start(bf16[128,768]{1,0:T(8,128)(2,1)} %param.8) | copy-start | bytes 589828
  10.2 13.4 %copy-start.5 = (f32[1,1,6]{2,1,0:T(1,128)S(1)}, f32[1,1,6]{2,1,0:T(1,128)}, u32[]{:S(2)}) copy-start(f32[1,1,6]{2,1,0:T(1,128)} %param.13) | copy-start | bytes 76
  11.1 181.9 %copy-start.1 = (bf16[1,256,768]{2,1,0:T(8,128)(2,1)S(1)}, bf16[1,256,768]{2,1,0:T(8,128)(2,1)}, u32[]{:S(2)}) copy-start(bf16[1,256,768]{2,1,0:T(8,128)(2,1)} %param.11) | copy-start | bytes 1179652
  11.1 183.0 %all-to-all-start = ((bf16[64,6,1,768]{3,1,2,0:T(8,128)(2,1)}), bf16[64,6,1,768]{3,1,2,0:T(8,128)(2,1)S(1)}, u32[]{:S(2)}, u32[]{:S(2)}) async-start(bf16[64,6,1,768]{3,1,2,0:T(8,128)(2,1)} %stack.2), calls=%async_computation | async-start | bytes 1572864 | tf_op jit(solution)/shard_map/all_to_all | solution.py:9
  22.9 255.7 %all-reduce.9.cloned.1.call-start = ((), (), s32[]{:S(2)}) async-start(), calls=%async_computation.2 | async-start | bytes 2359296 | tf_op jit(solution)/shard_map/psum | solution.py:31
  197.5 700.1 %all-reduce.7.cloned.1.call-start = ((), (), s32[]{:S(2)}) async-start(), calls=%async_computation.1 | async-start | bytes 4718592
  280.1 1.0 copy-start.2
  289.4 608.9 %copy-start.4 = (s32[1,1,6]{2,1,0:T(1,128)S(1)}, s32[1,1,6]{2,1,0:T(1,128)}, u32[]{:S(2)}) copy-start(s32[1,1,6]{2,1,0:T(1,128)} %param.12) | copy-start | bytes 76
Sparse Core Ops, SparseCore 0:
  197.6 81.0 all-reduce.8
  286.4 611.0 all-reduce.6
